TPU v7x, 32 devices: a whole 2x2x4 slice. The times are simulated.
32 devices in a mesh: tm: 16 (over z, y, core), head: 2 (over x).
Axes of the slice: x: 2, y: 2, z: 4, core: 2. Of those that a mesh axis runs over, the one named last changes fastest.
Arguments:
- frames: bfloat16 [32768, 1024], P('tm'), may hold values from -28 to 28
- w_query: bfloat16 [1024, 1024], P(None, 'head'), may hold values from -0.5 to 0.5
- w_key: bfloat16 [1024, 1024], P(None, 'head'), may hold values from -0.7 to 0.7
- w_value: bfloat16 [1024, 1024], P(None, 'head'), may hold values from -0.1875 to 0.1875
- w_out: bfloat16 [1024, 1024], replicated, may hold values from -0.5 to 0.5
Outputs:
- mixed: bfloat16 [32768, 1024], P('tm', 'head')
All inputs are finite; a program needn't handle non-finite values.
Results may differ from a plain program's by a relative error of at most 0.013.
Values may be sent and summed in bfloat16 or wider, within the bound.
A program may use at most 128 MiB of HBM per device.

v0:
```python
import jax
import jax.numpy as jnp
from jax import lax
from jax.sharding import PartitionSpec as P

DH = 64
WIN = 512
PK = 256


def from_behind(value, axis, steps):
    count = lax.axis_size(axis)
    leading, last = (max(0, -steps), min(count, count - steps))
    return lax.ppermute(value, axis, [(source, source + steps) for source in range(leading, last)])


def body(frames, w_query, w_key, w_value, w_out):
    block = frames.shape[0]
    width = w_query.shape[1]
    local_heads = width // DH
    blocks = lax.axis_size("tm")
    depth = 0
    while 2**depth < blocks:
        depth = depth + 1
    queries = jnp.dot(frames, w_query, preferred_element_type=jnp.float32).astype(jnp.bfloat16)
    keys = jnp.dot(frames, w_key, preferred_element_type=jnp.float32).astype(jnp.bfloat16)
    values = jnp.dot(frames, w_value, preferred_element_type=jnp.float32).astype(jnp.bfloat16)
    pooled_k = (
        keys.astype(jnp.float32).reshape(PK, block // PK, width).mean(axis=1).astype(jnp.bfloat16)
    )
    pooled_v = (
        values.astype(jnp.float32).reshape(PK, block // PK, width).mean(axis=1).astype(jnp.bfloat16)
    )
    here = lax.axis_index("tm")
    key_list = [keys]
    value_list = [values]
    rim_k, rim_v = from_behind((keys[block - WIN :], values[block - WIN :]), "tm", 1)
    every_k, every_v = (
        lax.all_gather(pooled_k, "tm", axis=0, tiled=True),
        lax.all_gather(pooled_v, "tm", axis=0, tiled=True),
    )
    key_list = key_list + [rim_k]
    value_list = value_list + [rim_v]
    for level in range(depth):
        source = jnp.maximum(here - 2**level, 0) * PK
        key_list.append(lax.dynamic_slice_in_dim(every_k, source, PK, 0))
        value_list.append(lax.dynamic_slice_in_dim(every_v, source, PK, 0))
    valid_list = [jnp.zeros((block,), dtype=bool), jnp.full((WIN,), here >= 1)]
    for level in range(depth):
        valid_list.append(jnp.full((PK,), here >= 2**level))
    outside = jnp.concatenate(valid_list, 0)
    all_k = jnp.concatenate(key_list, 0)
    all_v = jnp.concatenate(value_list, 0)
    total = all_k.shape[0]
    heads_k = all_k.reshape(total, local_heads, DH)
    heads_v = all_v.reshape(total, local_heads, DH)
    qrows = min(512, block)
    scale = DH ** (-0.5)
    kpos = jnp.arange(total, dtype=jnp.int32)
    outputs = []
    for sub in range(block // qrows):
        query_part = queries[sub * qrows : (sub + 1) * qrows].reshape(qrows, local_heads, DH)
        score = (
            jnp.einsum("qhd,khd->hqk", query_part, heads_k, preferred_element_type=jnp.float32)
            * scale
        )
        qpos = sub * qrows + jnp.arange(qrows, dtype=jnp.int32)
        causal = kpos[None, :] <= qpos[:, None]
        allowed = jnp.where(kpos[None, :] < block, causal, outside[None, :])
        score = jnp.where(allowed[None], score, jnp.float32(-1e30))
        top = jnp.max(score, axis=-1, keepdims=True)
        expo = jnp.where(allowed[None], jnp.exp(score - top), jnp.float32(0.0))
        weight = (expo / jnp.sum(expo, axis=-1, keepdims=True)).astype(jnp.bfloat16)
        context = jnp.einsum("hqk,khd->qhd", weight, heads_v, preferred_element_type=jnp.float32)
        outputs.append(context.reshape(qrows, width).astype(jnp.bfloat16))
    context = jnp.concatenate(outputs, 0)
    frame_rows = lax.all_to_all(context, "head", split_axis=0, concat_axis=1, tiled=True)
    projected = jnp.dot(frame_rows, w_out, preferred_element_type=jnp.float32).astype(jnp.bfloat16)
    return lax.all_to_all(projected, "head", split_axis=1, concat_axis=0, tiled=True)


def solution(mesh):
    in_specs = (P("tm", None), P(None, "head"), P(None, "head"), P(None, "head"), P())
    out_specs = P("tm", "head")
    return jax.shard_map(body, mesh=mesh, in_specs=in_specs, out_specs=out_specs, check_vma=False)
```

profile of v0, /device:TPU:0, one launch (start us, length us, event | category | flops | bytes accessed | tf_op | source)
XLA Modules:
  0.0 448.3 jit_solution(1765842533099350100)
XLA Ops:
  6.5 6.4 %constant_dynamic-update-slice_fusion.4 = (bf16[3584,512]{1,0:T(8,128)(2,1)}, bf16[2048,512]{1,0:T(8,128)(2,1)S(1)}) fusion(bf16[2048,1024]{1,0:T(8,128)(2,1)} %param.5, bf16[1024,512]{1,0:T(8,128)(2,1)} %param.7), kind=kOutput, calls=%fused_computation.73 | convolution fusion | flops 2148532224 | bytes 9437184 | tf_op jit(solution)/shard_map/dot_general | solution.py:26
  16.5 5.9 %constant_dynamic-update-slice_fusion.1 = (bf16[3584,512]{1,0:T(8,128)(2,1)}, bf16[2048,512]{1,0:T(8,128)(2,1)S(1)}) fusion(bf16[2048,1024]{1,0:T(8,128)(2,1)} %param.5, bf16[1024,512]{1,0:T(8,128)(2,1)S(1)} %copy-done.10), kind=kOutput, calls=%fused_computation.70 | convolution fusion | flops 2148532224 | bytes 9437184 | tf_op jit(solution)/shard_map/dot_general | solution.py:27
  27.8 2.4 collective-permute-start.1
  32.1 4.8 %collective-permute-start = (bf16[512,512]{1,0:T(8,128)(2,1)}, bf16[512,512]{1,0:T(8,128)(2,1)S(1)}, u32[]{:S(2)}, u32[]{:S(2)}) collective-permute-start(bf16[512,512]{1,0:T(8,128)(2,1)} %slice.24), channel_id=1, source_target_pairs={{0,2},{2,4},{4,6},{6,8},{8,10},{10,12},{12,14},{14,16},{16,18},{18... | collective-permute-start | bytes 1572872 | tf_op jit(solution)/shard_map/ppermute | solution.py:14
  38.2 8.2 %fusion.24 = (pred[512,3584]{1,0:T(8,128)(4,1)}, pred[512,3584]{1,0:T(8,128)(4,1)}, pred[512,3584]{1,0:T(8,128)(4,1)}, pred[512,3584]{1,0:T(8,128)(4,1)}) fusion(pred[3584]{0:T(1024)(128)(4,1)S(1)} %dynamic-update-slice.11, pred[3584]{0:T(1024)(128)(4,1)S(1)} %iota_compare_fusion.4, s32[512]{0:T(512)S(1)} %iota_add_fusion.2, s32[512]{0:T(512)S(1)} %get-tuple-element.28, ...), kind=kLoop, calls=%fused_computation.40 | loop fusion | flops 14680064 | bytes 7353344 | tf_op jit(solution)/shard_map/jit(_where)/select_n | solution.py:69
  46.4 3.8 convolution_convert_fusion.1
  50.2 2.9 fusion.48
  54.8 17.9 %all-gather.5.cloned.1.call-done = bf16[4096,512]{1,0:T(8,128)(2,1)} async-done(((bf16[256,512]{1,0:T(8,128)(2,1)}), bf16[4096,512]{1,0:T(8,128)(2,1)}) %all-gather.5.cloned.1.call-update) | async-done | bytes 4194320 | tf_op jit(solution)/shard_map/all_gather | solution.py:39
  72.7 51.2 %all-gather.3.cloned.1.call-done = bf16[4096,512]{1,0:T(8,128)(2,1)} async-done(((bf16[256,512]{1,0:T(8,128)(2,1)}), bf16[4096,512]{1,0:T(8,128)(2,1)}) %all-gather.3.cloned.1.call-update) | async-done | bytes 4194320 | tf_op jit(solution)/shard_map/all_gather | solution.py:40
  130.8 5.9 %copy.19 = bf16[3584,512]{0,1:T(8,128)(2,1)} copy(bf16[3584,512]{1,0:T(8,128)(2,1)} %dynamic-slice_dynamic-update-slice_fusion) | data formatting | bytes 7340032 | tf_op jit(solution)/shard_map/concatenate | solution.py:52
  141.9 6.0 %copy.18 = bf16[3584,512]{0,1:T(8,128)(2,1)} copy(bf16[3584,512]{1,0:T(8,128)(2,1)} %dynamic-slice_dynamic-update-slice_fusion.4) | data formatting | bytes 7340032 | tf_op jit(solution)/shard_map/concatenate | solution.py:53
  147.8 32.6 %fusion.52 = (f32[8,512]{1,0:T(8,128)S(1)}, f32[8,512,3584]{2,1,0:T(8,128)}) fusion(pred[512,3584]{1,0:T(8,128)(4,1)} %get-tuple-element.9, bf16[512,8,64]{0,2,1:T(8,128)(2,1)S(1)} %bitcast.70, bf16[3584,8,64]{0,2,1:T(8,128)(2,1)} %bitcast.53), kind=kOutput, calls=%fused_computation.90 | convolution fusion | flops 1952452096 | bytes 64765952 | tf_op jit(solution)/shard_map/sub | solution.py:72
  180.4 21.9 %fusion.39 = bf16[8,64,512]{2,1,0:T(8,128)(2,1)S(1)} fusion(bf16[3584,8,64]{0,2,1:T(8,128)(2,1)} %bitcast.57, f32[8,512,3584]{2,1,0:T(8,128)} %get-tuple-element.24, f32[8,512]{1,0:T(8,128)S(1)} %get-tuple-element.23), kind=kOutput, calls=%fused_computation.58 | convolution fusion | flops 1908670464 | bytes 62930944 | tf_op jit(solution)/shard_map/hqk,khd->qhd/dot_general | solution.py:74
  203.3 32.3 %fusion.51 = (f32[8,512]{1,0:T(8,128)S(1)}, f32[8,512,3584]{2,1,0:T(8,128)}) fusion(pred[512,3584]{1,0:T(8,128)(4,1)} %get-tuple-element.10, bf16[512,8,64]{0,2,1:T(8,128)(2,1)S(1)} %bitcast.69, bf16[3584,8,64]{0,2,1:T(8,128)(2,1)} %bitcast.54), kind=kOutput, calls=%fused_computation.89 | convolution fusion | flops 1952452096 | bytes 64765952 | tf_op jit(solution)/shard_map/sub | solution.py:72
  235.6 21.9 %fusion.38 = bf16[8,64,512]{2,1,0:T(8,128)(2,1)S(1)} fusion(bf16[3584,8,64]{0,2,1:T(8,128)(2,1)} %bitcast.58, f32[8,512,3584]{2,1,0:T(8,128)} %get-tuple-element.22, f32[8,512]{1,0:T(8,128)S(1)} %get-tuple-element.21), kind=kOutput, calls=%fused_computation.57 | convolution fusion | flops 1908670464 | bytes 62930944 | tf_op jit(solution)/shard_map/hqk,khd->qhd/dot_general | solution.py:74
  258.5 32.2 %fusion.50 = (f32[8,512]{1,0:T(8,128)S(1)}, f32[8,512,3584]{2,1,0:T(8,128)}) fusion(pred[512,3584]{1,0:T(8,128)(4,1)} %get-tuple-element.11, bf16[512,8,64]{0,2,1:T(8,128)(2,1)S(1)} %bitcast.68, bf16[3584,8,64]{0,2,1:T(8,128)(2,1)} %bitcast.55), kind=kOutput, calls=%fused_computation.88 | convolution fusion | flops 1952452096 | bytes 64765952 | tf_op jit(solution)/shard_map/sub | solution.py:72
  290.7 21.9 %fusion.37 = bf16[8,64,512]{2,1,0:T(8,128)(2,1)S(1)} fusion(bf16[3584,8,64]{0,2,1:T(8,128)(2,1)} %bitcast.59, f32[8,512,3584]{2,1,0:T(8,128)} %get-tuple-element.20, f32[8,512]{1,0:T(8,128)S(1)} %get-tuple-element.19), kind=kOutput, calls=%fused_computation.56 | convolution fusion | flops 1908670464 | bytes 62930944 | tf_op jit(solution)/shard_map/hqk,khd->qhd/dot_general | solution.py:74
  313.6 32.4 %fusion.49 = (f32[8,512]{1,0:T(8,128)S(1)}, f32[8,512,3584]{2,1,0:T(8,128)}) fusion(pred[512,3584]{1,0:T(8,128)(4,1)} %get-tuple-element.12, bf16[512,8,64]{0,2,1:T(8,128)(2,1)S(1)} %bitcast.67, bf16[3584,8,64]{0,2,1:T(8,128)(2,1)} %bitcast.56), kind=kOutput, calls=%fused_computation.87 | convolution fusion | flops 1952452096 | bytes 64765952 | tf_op jit(solution)/shard_map/sub | solution.py:72
  346.0 22.9 %fusion.36 = bf16[8,64,512]{2,1,0:T(8,128)(2,1)} fusion(bf16[3584,8,64]{0,2,1:T(8,128)(2,1)} %bitcast.60, f32[8,512,3584]{2,1,0:T(8,128)} %get-tuple-element.18, f32[8,512]{1,0:T(8,128)S(1)} %get-tuple-element.17), kind=kOutput, calls=%fused_computation.55 | convolution fusion | flops 1908670464 | bytes 62930944 | tf_op jit(solution)/shard_map/hqk,khd->qhd/dot_general | solution.py:74
  372.3 28.9 %all_to_all.38 = bf16[2,1024,512]{2,1,0:T(8,128)(2,1)} all-to-all(bf16[2,1024,512]{2,1,0:T(8,128)(2,1)S(1)} %bitcast.50), channel_id=1, replica_groups=mesh['tm'=16,'head'=2] {'head'}, dimensions={0} | all-to-all | bytes 4194304 | tf_op jit(solution)/shard_map/all_to_all | solution.py:77
  401.3 3.9 copy.24
  405.2 4.0 convolution_convert_fusion.3
  409.2 28.1 %all_to_all.39 = bf16[1024,2,512]{0,2,1:T(8,128)(2,1)} all-to-all(bf16[1024,2,512]{0,2,1:T(8,128)(2,1)S(1)} %bitcast.62), channel_id=1, replica_groups=mesh['tm'=16,'head'=2] {'head'}, dimensions={1} | all-to-all | bytes 4194304 | tf_op jit(solution)/shard_map/all_to_all | solution.py:79
  437.3 3.9 copy.25
  (64 shorter events, 32.2 us)
Async XLA Ops:
  6.5 398.7 %copy-start = (bf16[1024,1024]{1,0:T(8,128)(2,1)S(1)}, bf16[1024,1024]{1,0:T(8,128)(2,1)}, u32[]{:S(2)}) copy-start(bf16[1024,1024]{1,0:T(8,128)(2,1)} %param.9) | copy-start | bytes 6291460
  6.5 9.9 %copy-start.10 = (bf16[1024,512]{1,0:T(8,128)(2,1)S(1)}, bf16[1024,512]{1,0:T(8,128)(2,1)}, u32[]{:S(2)}) copy-start(bf16[1024,512]{1,0:T(8,128)(2,1)} %param.8) | copy-start | bytes 3145732
  6.5 66.2 %all-gather.5.cloned.1.call-start = ((), (), s32[]{:S(2)}) async-start(), calls=%async_computation.3 | async-start | bytes 4456448 | tf_op jit(solution)/shard_map/all_gather | solution.py:39
  12.9 1.3 copy-start.1
  16.4 107.5 %all-gather.3.cloned.1.call-start = ((), (), s32[]{:S(2)}) async-start(), calls=%async_computation.2 | async-start | bytes 4456448 | tf_op jit(solution)/shard_map/all_gather | solution.py:40
  22.4 1.3 copy-start.2
  27.8 25.3 %collective-permute-start.1 = (bf16[512,512]{1,0:T(8,128)(2,1)}, bf16[512,512]{1,0:T(8,128)(2,1)S(1)}, u32[]{:S(2)}, u32[]{:S(2)}) collective-permute-start(bf16[512,512]{1,0:T(8,128)(2,1)} %slice.26), channel_id=1, source_target_pairs={{0,2},{2,4},{4,6},{6,8},{8,10},{10,12},{12,14},{14,16},{16,18},{18... | collective-permute-start | bytes 1572872 | tf_op jit(solution)/shard_map/ppermute | solution.py:14
  32.1 21.9 %collective-permute-start = (bf16[512,512]{1,0:T(8,128)(2,1)}, bf16[512,512]{1,0:T(8,128)(2,1)S(1)}, u32[]{:S(2)}, u32[]{:S(2)}) collective-permute-start(bf16[512,512]{1,0:T(8,128)(2,1)} %slice.24), channel_id=1, source_target_pairs={{0,2},{2,4},{4,6},{6,8},{8,10},{10,12},{12,14},{14,16},{16,18},{18... | collective-permute-start | bytes 1572872 | tf_op jit(solution)/shard_map/ppermute | solution.py:14
  38.2 8.2 %copy-start.9 = (bf16[2048,1024]{1,0:T(8,128)(2,1)S(1)}, bf16[2048,1024]{1,0:T(8,128)(2,1)}, u32[]{:S(2)}) copy-start(bf16[2048,1024]{1,0:T(8,128)(2,1)} %param.5) | copy-start | bytes 12582916
  38.2 8.2 %copy-start.11 = (bf16[1024,512]{1,0:T(8,128)(2,1)S(1)}, bf16[1024,512]{1,0:T(8,128)(2,1)}, u32[]{:S(2)}) copy-start(bf16[1024,512]{1,0:T(8,128)(2,1)} %param.6) | copy-start | bytes 3145732
  138.4 9.4 %copy-start.8 = (bf16[512,512]{0,1:T(8,128)(2,1)S(1)}, bf16[512,512]{0,1:T(8,128)(2,1)}, u32[]{:S(2)}) copy-start(bf16[512,512]{0,1:T(8,128)(2,1)} %get-tuple-element.5) | copy-start | bytes 1572868
  180.4 22.9 %copy-start.7 = (bf16[512,512]{0,1:T(8,128)(2,1)S(1)}, bf16[512,512]{0,1:T(8,128)(2,1)}, u32[]{:S(2)}) copy-start(bf16[512,512]{0,1:T(8,128)(2,1)} %get-tuple-element.8) | copy-start | bytes 1572868
  235.6 22.9 %copy-start.6 = (bf16[512,512]{0,1:T(8,128)(2,1)S(1)}, bf16[512,512]{0,1:T(8,128)(2,1)}, u32[]{:S(2)}) copy-start(bf16[512,512]{0,1:T(8,128)(2,1)} %get-tuple-element.7) | copy-start | bytes 1572868
  290.7 22.9 %copy-start.5 = (bf16[512,512]{0,1:T(8,128)(2,1)S(1)}, bf16[512,512]{0,1:T(8,128)(2,1)}, u32[]{:S(2)}) copy-start(bf16[512,512]{0,1:T(8,128)(2,1)} %get-tuple-element.6) | copy-start | bytes 1572868
  346.0 24.9 %copy-start.3 = (bf16[512,512]{1,0:T(8,128)(2,1)S(1)}, bf16[512,512]{1,0:T(8,128)(2,1)}, u32[]{:S(2)}) copy-start(bf16[512,512]{1,0:T(8,128)(2,1)} %copy.20) | copy-start | bytes 1572868
  346.0 24.9 %copy-start.4 = (bf16[512,512]{1,0:T(8,128)(2,1)S(1)}, bf16[512,512]{1,0:T(8,128)(2,1)}, u32[]{:S(2)}) copy-start(bf16[512,512]{1,0:T(8,128)(2,1)} %copy.21) | copy-start | bytes 1572868
Sparse Core Ops, SparseCore 0:
  16.6 56.1 all-gather.4
  74.9 48.9 all-gather.2
where the time goes:
time: 455 us; the launch traced here: 448 us
  matrix products  238 us (52%)
  waiting for transfers between devices  69.2 us (15%)
  blocking collectives  57.1 us (13%)
  local copies, waits for them, and re-layouts  49.1 us (11%)
  other arithmetic  13.9 us (3%)
  between operations  13.8 us (3%)
  starting transfers between devices  7.22 us (2%)
    sub x4, matrix products, body(): expo = jnp.where(allowed[None], jnp.exp(score - top), jnp.float32(0.0))  130 us
    dot_general x4, matrix products, body(): jnp.einsum('hqk,khd->qhd', weight, heads_v, preferred_element_type=jnp.fl...  88.5 us
    all_gather x1, waiting for transfers between devices, body(): lax.all_gather(pooled_v, 'tm', axis=0, tiled=True)  51.2 us
    all_to_all x1, blocking collectives, body(): lax.all_to_all(context, 'head', split_axis=0, concat_axis=1, tiled=True)  28.9 us
    all_to_all x1, blocking collectives, body(): lax.all_to_all(projected, 'head', split_axis=1, concat_axis=0, tiled=True)  28.1 us
    all_gather x1, waiting for transfers between devices, body(): lax.all_gather(pooled_k, 'tm', axis=0, tiled=True)  17.9 us
    unnamed x36, local copies, waits for them, and re-layouts  13.9 us
  transfers between devices with their start and end apart: 4, of which 2 were waited for; matrix products, arithmetic and copies ran while one was open for 7% of the time, Pallas kernels for 0%

commit v1 on v0

v1 whole, which is shorter than its diff:
```python
import functools
import math

import jax
import jax.numpy as jnp
from jax import lax
from jax.experimental import pallas as pl
from jax.experimental.pallas import tpu as pltpu
from jax.sharding import PartitionSpec as P

DH = 64
WIN = 512
PK = 256
SUMS = 16
STATE = DH + SUMS + 8
BQ = 512
BK = 512
NEG = -1e30


def step(k, q, v, state, mask=None):
    top, acc = state
    s = jnp.dot(k, q, preferred_element_type=jnp.float32)
    if mask is not None:
        s = jnp.where(mask, s, NEG)
    here = jnp.max(s, axis=0, keepdims=True)
    if top is None:
        p = jnp.exp2(s - here).astype(jnp.bfloat16)
        return here, jnp.dot(v, p, preferred_element_type=jnp.float32)
    new = jnp.maximum(top, here)
    p = jnp.exp2(s - new).astype(jnp.bfloat16)
    acc = acc * jnp.exp2(top - new) + jnp.dot(v, p, preferred_element_type=jnp.float32)
    return new, acc


def head_queries(q):
    first = lax.broadcasted_iota(jnp.int32, q.shape, 0) < DH
    zero = jnp.zeros_like(q)
    return jnp.where(first, q, zero), jnp.where(first, zero, q)


def local_kernel(q_ref, k_ref, v_ref, out_ref):
    index = pl.program_id(1)
    bq = q_ref.shape[1]
    qs = head_queries(q_ref[...])
    ones = jnp.ones((SUMS, bq), jnp.bfloat16)

    def tile(j, states, mask):
        rows = pl.ds(pl.multiple_of(j * bq, bq), bq)
        k = k_ref[rows, :]
        result = []
        for h in range(2):
            v = jnp.concatenate([v_ref[h * DH : (h + 1) * DH, rows], ones], 0)
            result.append(step(k, qs[h], v, states[h], mask))
        return tuple(result)

    mask = lax.broadcasted_iota(jnp.int32, (bq, bq), 0) <= lax.broadcasted_iota(
        jnp.int32, (bq, bq), 1
    )
    states = tile(index, ((None, None), (None, None)), mask)
    states = lax.fori_loop(0, index, lambda j, st: tile(j, st, None), states)
    for h in range(2):
        top, acc = states[h]
        out_ref[h, : DH + SUMS] = acc
        out_ref[h, DH + SUMS :] = jnp.broadcast_to(top, (8, bq))


def remote_kernel(q_ref, state_ref, k_ref, v_ref, ones_ref, out_ref):
    qs = head_queries(q_ref[...])
    total = k_ref.shape[0]
    states = [
        (state_ref[h, DH + SUMS : DH + SUMS + 1], state_ref[h, : DH + SUMS]) for h in range(2)
    ]
    for start in range(0, total, BK):
        stop = min(total, start + BK)
        k = k_ref[start:stop]
        for h in range(2):
            v = jnp.concatenate(
                [v_ref[h * DH : (h + 1) * DH, start:stop], ones_ref[:, start:stop]], 0
            )
            states[h] = step(k, qs[h], v, states[h])
    for h in range(2):
        acc = states[h][1]
        out_ref[h * DH : (h + 1) * DH] = (acc[:DH] / acc[DH : DH + 1]).astype(jnp.bfloat16)


def local_attention(q_t, keys, v_t):
    width, block = q_t.shape
    pairs = width // (2 * DH)
    bq = min(BQ, block)
    return pl.pallas_call(
        local_kernel,
        grid=(pairs, block // bq),
        in_specs=[
            pl.BlockSpec((2 * DH, bq), lambda p, i: (p, i)),
            pl.BlockSpec((block, 2 * DH), lambda p, i: (0, p)),
            pl.BlockSpec((2 * DH, block), lambda p, i: (p, 0)),
        ],
        out_specs=pl.BlockSpec((2, STATE, bq), lambda p, i: (p, 0, i)),
        out_shape=jax.ShapeDtypeStruct((2 * pairs, STATE, block), jnp.float32),
        compiler_params=pltpu.CompilerParams(vmem_limit_bytes=48 * 2**20),
        cost_estimate=pl.CostEstimate(
            flops=8 * width * block * block, bytes_accessed=8 * width * block, transcendentals=0
        ),
    )(q_t, keys, v_t)


def remote_attention(chunk, q_t, state, keys, v_t, ones):
    width, block = q_t.shape
    pairs = width // (2 * DH)
    bq = min(BQ, block)
    total = keys.shape[0]
    return pl.pallas_call(
        remote_kernel,
        grid=(pairs,),
        in_specs=[
            pl.BlockSpec((2 * DH, bq), lambda p: (p, chunk)),
            pl.BlockSpec((2, STATE, bq), lambda p: (p, 0, chunk)),
            pl.BlockSpec((total, 2 * DH), lambda p: (0, p)),
            pl.BlockSpec((2 * DH, total), lambda p: (p, 0)),
            pl.BlockSpec((SUMS, total), lambda p: (0, 0)),
        ],
        out_specs=pl.BlockSpec((2 * DH, bq), lambda p: (p, 0)),
        out_shape=jax.ShapeDtypeStruct((width, bq), jnp.bfloat16),
        compiler_params=pltpu.CompilerParams(vmem_limit_bytes=48 * 2**20),
        cost_estimate=pl.CostEstimate(
            flops=16 * width * bq * total, bytes_accessed=8 * width * total, transcendentals=0
        ),
    )(q_t, state, keys, v_t, ones)


def from_behind(value, steps):
    count = lax.axis_size("tm")
    return lax.ppermute(value, "tm", [(s, s + steps) for s in range(count - steps)])


def body(frames, w_query, w_key, w_value, w_out):
    block = frames.shape[0]
    width = w_query.shape[1]
    blocks = lax.axis_size("tm")
    sides = lax.axis_size("head")
    depth = 0
    while 2**depth < blocks:
        depth = depth + 1
    here = lax.axis_index("tm")
    side = lax.axis_index("head")
    across = (((0,), (1,)), ((), ()))
    keys = jnp.dot(frames, w_key, preferred_element_type=jnp.float32).astype(jnp.bfloat16)
    v_t = lax.dot_general(w_value, frames, across, preferred_element_type=jnp.float32).astype(
        jnp.bfloat16
    )
    factor = DH**-0.5 * math.log2(math.e)
    q_t = (
        lax.dot_general(w_query, frames, across, preferred_element_type=jnp.float32) * factor
    ).astype(jnp.bfloat16)
    span = block // PK
    pool = jnp.where(
        jnp.arange(block)[:, None] // span == jnp.arange(PK)[None, :], 1.0 / span, 0.0
    ).astype(jnp.bfloat16)
    pooled_k = lax.dot_general(
        pool, keys, (((0,), (0,)), ((), ())), preferred_element_type=jnp.float32
    ).astype(jnp.bfloat16)
    pooled_v = jnp.dot(v_t, pool, preferred_element_type=jnp.float32).astype(jnp.bfloat16)

    got_k = [from_behind(keys[block - WIN :], 1)]
    got_v = [from_behind(v_t[:, block - WIN :], 1)]
    valid = [jnp.full((WIN,), here >= 1)]
    for level in range(depth):
        got_k.append(from_behind(pooled_k, 2**level))
        got_v.append(from_behind(pooled_v, 2**level))
        valid.append(jnp.full((PK,), here >= 2**level))
    valid = jnp.concatenate(valid, 0)
    state = local_attention(q_t, keys, v_t)
    far_k = jnp.where(valid[:, None], jnp.concatenate(got_k, 0), keys[:1])
    far_v = jnp.concatenate(got_v, 1)
    ones = jnp.broadcast_to(valid[None, :], (SUMS, valid.shape[0])).astype(jnp.bfloat16)

    mine = lax.dynamic_slice_in_dim(w_out, side * width, width, 1)
    w_rows = [
        lax.dynamic_slice_in_dim(mine, ((side + s) % sides) * width, width, 0)
        for s in range(sides)
    ]
    bq = min(BQ, block)
    outputs = []
    for chunk in range(block // bq):
        part = remote_attention(chunk, q_t, state, far_k, far_v, ones)
        total = lax.dot_general(
            part, w_rows[0], (((0,), (0,)), ((), ())), preferred_element_type=jnp.float32
        )
        for s in range(1, sides):
            other = lax.ppermute(
                part, "head", [((d + s) % sides, d) for d in range(sides)]
            )
            total = total + lax.dot_general(
                other, w_rows[s], (((0,), (0,)), ((), ())), preferred_element_type=jnp.float32
            )
        outputs.append(total.astype(jnp.bfloat16))
    return jnp.concatenate(outputs, 0)


def solution(mesh):
    in_specs = (P("tm", None), P(None, "head"), P(None, "head"), P(None, "head"), P())
    out_specs = P("tm", "head")
    return jax.shard_map(body, mesh=mesh, in_specs=in_specs, out_specs=out_specs, check_vma=False)
```

time: 455 us -> 196 us (0.43)
  the two profiles are of different devices: /device:TPU:0 before, /device:TPU:13 now
where the time goes in v1:
time: 196 us
  Pallas kernels  98.2 us (50%)
  waiting for transfers between devices  41.8 us (21%)
  starting transfers between devices  27.8 us (14%)
  matrix products  19.7 us (10%)
  local copies, waits for them, and re-layouts  6.29 us (3%)
    pallas_call x4, Pallas kernels, remote_attention(): pl.pallas_call(remote_kernel, grid=(pairs,), in_specs=[pl.BlockSpec((2 *...  53.2 us
    pallas_call x1, Pallas kernels, local_attention(): pl.pallas_call(local_kernel, grid=(pairs, block // bq), in_specs=[pl.Bloc...  45 us
    ppermute x10, starting transfers between devices, from_behind(): lax.ppermute(value, 'tm', [(s, s + steps) for s in range(count - steps)])  24.7 us
    ppermute x4, waiting for transfers between devices, body(): lax.ppermute(part, 'head', [((d + s) % sides, d) for d in range(sides)])  22 us
    ppermute x10, waiting for transfers between devices, from_behind(): lax.ppermute(value, 'tm', [(s, s + steps) for s in range(count - steps)])  19.7 us
    dot_general x1, matrix products, body(): jnp.dot(frames, w_key, preferred_element_type=jnp.float32)  4.98 us
    unnamed x28, local copies, waits for them, and re-layouts  4.03 us
  transfers between devices with their start and end apart: 14, of which 4 were waited for; matrix products, arithmetic and copies ran while one was open for 9% of the time, Pallas kernels for 30%

profile of v1, /device:TPU:13, one launch (start us, length us, event | category | flops | bytes accessed | tf_op | source)
XLA Modules:
  0.0 195.9 jit_solution(17906855430347383438)
XLA Ops:
  0.0 5.0 %convolution_convert_fusion.1.k_ref = bf16[2048,512]{1,0:T(8,128)(2,1)S(1)} fusion(bf16[2048,1024]{1,0:T(8,128)(2,1)} %param.5, bf16[1024,512]{1,0:T(8,128)(2,1)} %param.7), kind=kOutput, calls=%fused_computation.2 | convolution fusion | flops 2148532224 | bytes 7340032 | tf_op jit(solution)/shard_map/dot_general | solution.py:148
  5.0 2.1 %fusion.6 = bf16[256,512]{1,0:T(8,128)(2,1)} fusion(bf16[2048,512]{1,0:T(8,128)(2,1)S(1)} %convolution_convert_fusion.1.k_ref, s32[2048]{0:T(1024)S(1)} %add_select_fusion), kind=kOutput, calls=%fused_computation.17 | convolution fusion | flops 538574848 | bytes 2367488 | tf_op jit(solution)/shard_map/dot_general | solution.py:160
  7.1 3.7 %collective-permute-start.1 = (bf16[256,512]{1,0:T(8,128)(2,1)}, bf16[256,512]{1,0:T(8,128)(2,1)}, u32[]{:S(2)}, u32[]{:S(2)}) collective-permute-start(bf16[256,512]{1,0:T(8,128)(2,1)} %fusion.6), channel_id=1, source_target_pairs={{0,2},{2,4},{4,6},{6,8},{8,10},{10,12},{12,14},{14,16},{16,18},{18... | collective-permute-start | bytes 786440 | tf_op jit(solution)/shard_map/ppermute | solution.py:134
  10.8 3.1 %collective-permute-start.2 = (bf16[256,512]{1,0:T(8,128)(2,1)}, bf16[256,512]{1,0:T(8,128)(2,1)}, u32[]{:S(2)}, u32[]{:S(2)}) collective-permute-start(bf16[256,512]{1,0:T(8,128)(2,1)} %fusion.6), channel_id=1, source_target_pairs={{0,4},{2,6},{4,8},{6,10},{8,12},{10,14},{12,16},{14,18},{16,20},{1... | collective-permute-start | bytes 786440 | tf_op jit(solution)/shard_map/ppermute | solution.py:134
  14.0 3.2 %collective-permute-start.3 = (bf16[256,512]{1,0:T(8,128)(2,1)}, bf16[256,512]{1,0:T(8,128)(2,1)}, u32[]{:S(2)}, u32[]{:S(2)}) collective-permute-start(bf16[256,512]{1,0:T(8,128)(2,1)} %fusion.6), channel_id=1, source_target_pairs={{0,8},{2,10},{4,12},{6,14},{8,16},{10,18},{12,20},{14,22},{16,24},... | collective-permute-start | bytes 786440 | tf_op jit(solution)/shard_map/ppermute | solution.py:134
  19.4 2.8 %collective-permute-start = (bf16[512,512]{1,0:T(8,128)(2,1)}, bf16[512,512]{1,0:T(8,128)(2,1)S(1)}, u32[]{:S(2)}, u32[]{:S(2)}) collective-permute-start(bf16[512,512]{1,0:T(8,128)(2,1)} %slice.12), channel_id=1, source_target_pairs={{0,2},{2,4},{4,6},{6,8},{8,10},{10,12},{12,14},{14,16},{16,18},{18... | collective-permute-start | bytes 1572872 | tf_op jit(solution)/shard_map/ppermute | solution.py:134
  22.2 3.7 %convolution_convert_fusion.v_ref = bf16[512,2048]{1,0:T(8,128)(2,1)} fusion(bf16[1024,512]{1,0:T(8,128)(2,1)S(1)} %copy-done.5, bf16[2048,1024]{1,0:T(8,128)(2,1)S(1)} %copy-done.4), kind=kOutput, calls=%fused_computation.1 | convolution fusion | flops 2148532224 | bytes 7340032 | tf_op jit(solution)/shard_map/dot_general | solution.py:149
  25.9 2.4 %multiply_convert_fusion.q_ref = bf16[512,2048]{1,0:T(8,128)(2,1)S(1)} fusion(bf16[1024,512]{1,0:T(8,128)(2,1)S(1)} %copy-done.6, bf16[2048,1024]{1,0:T(8,128)(2,1)S(1)} %copy-done.4), kind=kOutput, calls=%fused_computation | convolution fusion | flops 2149580800 | bytes 7340032 | tf_op jit(solution)/shard_map/dot_general | solution.py:154
  28.3 45.0 %shard_map.55.state_ref = f32[8,88,2048]{2,1,0:T(8,128)} custom-call(bf16[512,2048]{1,0:T(8,128)(2,1)S(1)} %multiply_convert_fusion.q_ref, bf16[2048,512]{1,0:T(8,128)(2,1)S(1)} %convolution_convert_fusion.1.k_ref, bf16[512,2048]{1,0:T(8,128)(2,1)} %convolution_convert_fusion.v_ref), custom_call_target="tpu_custom_call" | custom-call | flops 17179869184 | bytes 8388608 | tf_op jit(solution)/shard_map/pallas_call | solution.py:91
  73.3 1.5 fusion.7
  77.2 2.1 %collective-permute-start.6 = (bf16[512,256]{1,0:T(8,128)(2,1)}, bf16[512,256]{1,0:T(8,128)(2,1)S(1)}, u32[]{:S(2)}, u32[]{:S(2)}) collective-permute-start(bf16[512,256]{1,0:T(8,128)(2,1)} %fusion.7), channel_id=1, source_target_pairs={{0,2},{2,4},{4,6},{6,8},{8,10},{10,12},{12,14},{14,16},{16,18},{18... | collective-permute-start | bytes 786440 | tf_op jit(solution)/shard_map/ppermute | solution.py:134
  79.4 2.9 %collective-permute-start.7 = (bf16[512,256]{1,0:T(8,128)(2,1)}, bf16[512,256]{1,0:T(8,128)(2,1)S(1)}, u32[]{:S(2)}, u32[]{:S(2)}) collective-permute-start(bf16[512,256]{1,0:T(8,128)(2,1)} %fusion.7), channel_id=1, source_target_pairs={{0,4},{2,6},{4,8},{6,10},{8,12},{10,14},{12,16},{14,18},{16,20},{1... | collective-permute-start | bytes 786440 | tf_op jit(solution)/shard_map/ppermute | solution.py:134
  83.3 1.9 collective-permute-start.8
  86.2 1.3 collective-permute-start.9
  88.5 2.4 %collective-permute-start.5 = (bf16[512,512]{1,0:T(8,128)(2,1)S(1)}, bf16[512,512]{1,0:T(8,128)(2,1)S(1)}, u32[]{:S(2)}, u32[]{:S(2)}) collective-permute-start(bf16[512,512]{1,0:T(8,128)(2,1)S(1)} %slice.14), channel_id=1, source_target_pairs={{0,2},{2,4},{4,6},{6,8},{8,10},{10,12},{12,14},{14,16},{16,18},{18... | collective-permute-start | bytes 1572872 | tf_op jit(solution)/shard_map/ppermute | solution.py:134
  91.2 19.7 %collective-permute-done.5 = bf16[512,512]{1,0:T(8,128)(2,1)S(1)} collective-permute-done((bf16[512,512]{1,0:T(8,128)(2,1)S(1)}, bf16[512,512]{1,0:T(8,128)(2,1)S(1)}, u32[]{:S(2)}, u32[]{:S(2)}) %collective-permute-start.5) | collective-permute-done | bytes 524320 | tf_op jit(solution)/shard_map/ppermute | solution.py:134
  111.2 13.2 %shard_map.56 = bf16[512,512]{1,0:T(8,128)(2,1)S(1)} custom-call(bf16[512,2048]{1,0:T(8,128)(2,1)S(1)} %copy-done.2, f32[8,88,2048]{2,1,0:T(8,128)} %shard_map.55.state_ref, bf16[1536,512]{1,0:T(8,128)(2,1)S(1)} %broadcast_select_fusion.k_ref, bf16[512,1536]{1,0:T(8,128)(2,1)S(1)} %constant_dynamic-update-slice_fusion.5.v_ref, ...), custom_call_target="tpu_custom_call" | custom-call | flops 6442450944 | bytes 6291456 | tf_op jit(solution)/shard_map/pallas_call | solution.py:113
  124.4 13.2 %shard_map.57 = bf16[512,512]{1,0:T(8,128)(2,1)S(1)} custom-call(bf16[512,2048]{1,0:T(8,128)(2,1)S(1)} %copy-done.2, f32[8,88,2048]{2,1,0:T(8,128)} %shard_map.55.state_ref, bf16[1536,512]{1,0:T(8,128)(2,1)S(1)} %broadcast_select_fusion.k_ref, bf16[512,1536]{1,0:T(8,128)(2,1)S(1)} %constant_dynamic-update-slice_fusion.5.v_ref, ...), custom_call_target="tpu_custom_call" | custom-call | flops 6442450944 | bytes 6291456 | tf_op jit(solution)/shard_map/pallas_call | solution.py:113
  137.6 13.2 %shard_map.58 = bf16[512,512]{1,0:T(8,128)(2,1)S(1)} custom-call(bf16[512,2048]{1,0:T(8,128)(2,1)S(1)} %copy-done.2, f32[8,88,2048]{2,1,0:T(8,128)} %shard_map.55.state_ref, bf16[1536,512]{1,0:T(8,128)(2,1)S(1)} %broadcast_select_fusion.k_ref, bf16[512,1536]{1,0:T(8,128)(2,1)S(1)} %constant_dynamic-update-slice_fusion.5.v_ref, ...), custom_call_target="tpu_custom_call" | custom-call | flops 6442450944 | bytes 6291456 | tf_op jit(solution)/shard_map/pallas_call | solution.py:113
  153.6 13.5 %shard_map.59 = bf16[512,512]{1,0:T(8,128)(2,1)S(1)} custom-call(bf16[512,2048]{1,0:T(8,128)(2,1)S(1)} %copy-done.2, f32[8,88,2048]{2,1,0:T(8,128)} %shard_map.55.state_ref, bf16[1536,512]{1,0:T(8,128)(2,1)S(1)} %broadcast_select_fusion.k_ref, bf16[512,1536]{1,0:T(8,128)(2,1)S(1)} %constant_dynamic-update-slice_fusion.5.v_ref, ...), custom_call_target="tpu_custom_call" | custom-call | flops 6442450944 | bytes 6291456 | tf_op jit(solution)/shard_map/pallas_call | solution.py:113
  168.6 7.5 %collective-permute-done.11 = bf16[512,512]{1,0:T(8,128)(2,1)S(1)} collective-permute-done((bf16[512,512]{1,0:T(8,128)(2,1)S(1)}, bf16[512,512]{1,0:T(8,128)(2,1)S(1)}, u32[]{:S(2)}, u32[]{:S(2)}) %collective-permute-start.11) | collective-permute-done | bytes 524320 | tf_op jit(solution)/shard_map/ppermute | solution.py:191
  177.4 10.0 %collective-permute-done.12 = bf16[512,512]{1,0:T(8,128)(2,1)S(1)} collective-permute-done((bf16[512,512]{1,0:T(8,128)(2,1)S(1)}, bf16[512,512]{1,0:T(8,128)(2,1)S(1)}, u32[]{:S(2)}, u32[]{:S(2)}) %collective-permute-start.12) | collective-permute-done | bytes 524320 | tf_op jit(solution)/shard_map/ppermute | solution.py:191
  188.6 4.5 %collective-permute-done.13 = bf16[512,512]{1,0:T(8,128)(2,1)S(1)} collective-permute-done((bf16[512,512]{1,0:T(8,128)(2,1)S(1)}, bf16[512,512]{1,0:T(8,128)(2,1)S(1)}, u32[]{:S(2)}, u32[]{:S(2)}) %collective-permute-start.13) | collective-permute-done | bytes 524320 | tf_op jit(solution)/shard_map/ppermute | solution.py:191
  194.4 1.5 pad_maximum_fusion
  (67 shorter events, 15.9 us)
Async XLA Ops:
  0.0 167.4 %copy-start = (bf16[1024,1024]{1,0:T(8,128)(2,1)S(1)}, bf16[1024,1024]{1,0:T(8,128)(2,1)}, u32[]{:S(2)}) copy-start(bf16[1024,1024]{1,0:T(8,128)(2,1)} %param.9) | copy-start | bytes 6291460
  0.0 22.2 %copy-start.5 = (bf16[1024,512]{1,0:T(8,128)(2,1)S(1)}, bf16[1024,512]{1,0:T(8,128)(2,1)}, u32[]{:S(2)}) copy-start(bf16[1024,512]{1,0:T(8,128)(2,1)} %param.8) | copy-start | bytes 3145732
  5.0 17.2 %copy-start.4 = (bf16[2048,1024]{1,0:T(8,128)(2,1)S(1)}, bf16[2048,1024]{1,0:T(8,128)(2,1)}, u32[]{:S(2)}) copy-start(bf16[2048,1024]{1,0:T(8,128)(2,1)} %param.5) | copy-start | bytes 12582916
  7.1 72.2 %collective-permute-start.1 = (bf16[256,512]{1,0:T(8,128)(2,1)}, bf16[256,512]{1,0:T(8,128)(2,1)}, u32[]{:S(2)}, u32[]{:S(2)}) collective-permute-start(bf16[256,512]{1,0:T(8,128)(2,1)} %fusion.6), channel_id=1, source_target_pairs={{0,2},{2,4},{4,6},{6,8},{8,10},{10,12},{12,14},{14,16},{16,18},{18... | collective-permute-start | bytes 786440 | tf_op jit(solution)/shard_map/ppermute | solution.py:134
  10.8 72.4 %collective-permute-start.2 = (bf16[256,512]{1,0:T(8,128)(2,1)}, bf16[256,512]{1,0:T(8,128)(2,1)}, u32[]{:S(2)}, u32[]{:S(2)}) collective-permute-start(bf16[256,512]{1,0:T(8,128)(2,1)} %fusion.6), channel_id=1, source_target_pairs={{0,4},{2,6},{4,8},{6,10},{8,12},{10,14},{12,16},{14,18},{16,20},{1... | collective-permute-start | bytes 786440 | tf_op jit(solution)/shard_map/ppermute | solution.py:134
  14.0 72.2 %collective-permute-start.3 = (bf16[256,512]{1,0:T(8,128)(2,1)}, bf16[256,512]{1,0:T(8,128)(2,1)}, u32[]{:S(2)}, u32[]{:S(2)}) collective-permute-start(bf16[256,512]{1,0:T(8,128)(2,1)} %fusion.6), channel_id=1, source_target_pairs={{0,8},{2,10},{4,12},{6,14},{8,16},{10,18},{12,20},{14,22},{16,24},... | collective-permute-start | bytes 786440 | tf_op jit(solution)/shard_map/ppermute | solution.py:134
  17.2 71.3 %collective-permute-start.4 = (bf16[256,512]{1,0:T(8,128)(2,1)}, bf16[256,512]{1,0:T(8,128)(2,1)S(1)}, u32[]{:S(2)}, u32[]{:S(2)}) collective-permute-start(bf16[256,512]{1,0:T(8,128)(2,1)} %fusion.6), channel_id=1, source_target_pairs={{0,16},{2,18},{4,20},{6,22},{8,24},{10,26},{12,28},{14,30},{1,17},... | collective-permute-start | bytes 786440 | tf_op jit(solution)/shard_map/ppermute | solution.py:134
  19.4 6.5 %copy-start.6 = (bf16[1024,512]{1,0:T(8,128)(2,1)S(1)}, bf16[1024,512]{1,0:T(8,128)(2,1)}, u32[]{:S(2)}) copy-start(bf16[1024,512]{1,0:T(8,128)(2,1)} %param.6) | copy-start | bytes 3145732
  19.4 57.8 %collective-permute-start = (bf16[512,512]{1,0:T(8,128)(2,1)}, bf16[512,512]{1,0:T(8,128)(2,1)S(1)}, u32[]{:S(2)}, u32[]{:S(2)}) collective-permute-start(bf16[512,512]{1,0:T(8,128)(2,1)} %slice.12), channel_id=1, source_target_pairs={{0,2},{2,4},{4,6},{6,8},{8,10},{10,12},{12,14},{14,16},{16,18},{18... | collective-permute-start | bytes 1572872 | tf_op jit(solution)/shard_map/ppermute | solution.py:134
  28.3 45.0 %copy-start.1 = (bf16[512,2048]{1,0:T(8,128)(2,1)}, bf16[512,2048]{1,0:T(8,128)(2,1)S(1)}, u32[]{:S(2)}) copy-start(bf16[512,2048]{1,0:T(8,128)(2,1)S(1)} %multiply_convert_fusion.q_ref) | copy-start | bytes 6291460
  28.3 45.0 %copy-start.3 = (bf16[512,2048]{1,0:T(8,128)(2,1)S(1)}, bf16[512,2048]{1,0:T(8,128)(2,1)}, u32[]{:S(2)}) copy-start(bf16[512,2048]{1,0:T(8,128)(2,1)} %convolution_convert_fusion.v_ref) | copy-start | bytes 6291460
  77.2 8.9 %copy-start.7 = (bf16[512,256]{1,0:T(8,128)(2,1)S(1)}, bf16[512,256]{1,0:T(8,128)(2,1)}, u32[]{:S(2)}) copy-start(bf16[512,256]{1,0:T(8,128)(2,1)} %fusion.7) | copy-start | bytes 786436
  77.2 33.7 %collective-permute-start.6 = (bf16[512,256]{1,0:T(8,128)(2,1)}, bf16[512,256]{1,0:T(8,128)(2,1)S(1)}, u32[]{:S(2)}, u32[]{:S(2)}) collective-permute-start(bf16[512,256]{1,0:T(8,128)(2,1)} %fusion.7), channel_id=1, source_target_pairs={{0,2},{2,4},{4,6},{6,8},{8,10},{10,12},{12,14},{14,16},{16,18},{18... | collective-permute-start | bytes 786440 | tf_op jit(solution)/shard_map/ppermute | solution.py:134
  79.4 31.7 %collective-permute-start.7 = (bf16[512,256]{1,0:T(8,128)(2,1)}, bf16[512,256]{1,0:T(8,128)(2,1)S(1)}, u32[]{:S(2)}, u32[]{:S(2)}) collective-permute-start(bf16[512,256]{1,0:T(8,128)(2,1)} %fusion.7), channel_id=1, source_target_pairs={{0,4},{2,6},{4,8},{6,10},{8,12},{10,14},{12,16},{14,18},{16,20},{1... | collective-permute-start | bytes 786440 | tf_op jit(solution)/shard_map/ppermute | solution.py:134
  83.3 27.8 %collective-permute-start.8 = (bf16[512,256]{1,0:T(8,128)(2,1)}, bf16[512,256]{1,0:T(8,128)(2,1)S(1)}, u32[]{:S(2)}, u32[]{:S(2)}) collective-permute-start(bf16[512,256]{1,0:T(8,128)(2,1)} %fusion.7), channel_id=1, source_target_pairs={{0,8},{2,10},{4,12},{6,14},{8,16},{10,18},{12,20},{14,22},{16,24},... | collective-permute-start | bytes 786440 | tf_op jit(solution)/shard_map/ppermute | solution.py:134
  86.2 24.9 %collective-permute-start.9 = (bf16[512,256]{1,0:T(8,128)(2,1)S(1)}, bf16[512,256]{1,0:T(8,128)(2,1)S(1)}, u32[]{:S(2)}, u32[]{:S(2)}) collective-permute-start(bf16[512,256]{1,0:T(8,128)(2,1)S(1)} %copy-done.7), channel_id=1, source_target_pairs={{0,16},{2,18},{4,20},{6,22},{8,24},{10,26},{12,28},{14,30},{1,17},... | collective-permute-start | bytes 786440 | tf_op jit(solution)/shard_map/ppermute | solution.py:134
  88.5 22.5 %collective-permute-start.5 = (bf16[512,512]{1,0:T(8,128)(2,1)S(1)}, bf16[512,512]{1,0:T(8,128)(2,1)S(1)}, u32[]{:S(2)}, u32[]{:S(2)}) collective-permute-start(bf16[512,512]{1,0:T(8,128)(2,1)S(1)} %slice.14), channel_id=1, source_target_pairs={{0,2},{2,4},{4,6},{6,8},{8,10},{10,12},{12,14},{14,16},{16,18},{18... | collective-permute-start | bytes 1572872 | tf_op jit(solution)/shard_map/ppermute | solution.py:134
  91.2 19.9 %copy-start.2 = (bf16[512,2048]{1,0:T(8,128)(2,1)S(1)}, bf16[512,2048]{1,0:T(8,128)(2,1)}, u32[]{:S(2)}) copy-start(bf16[512,2048]{1,0:T(8,128)(2,1)} %copy-done.1) | copy-start | bytes 6291460
  150.8 16.5 %collective-permute-start.10 = (bf16[512,512]{1,0:T(8,128)(2,1)S(1)}, bf16[512,512]{1,0:T(8,128)(2,1)S(1)}, u32[]{:S(2)}, u32[]{:S(2)}) collective-permute-start(bf16[512,512]{1,0:T(8,128)(2,1)S(1)} %shard_map.56), channel_id=1, source_target_pairs={{1,0},{0,1},{3,2},{2,3},{5,4},{4,5},{7,6},{6,7},{9,8},{8,9},{11,10... | collective-permute-start | bytes 1572872 | tf_op jit(solution)/shard_map/ppermute | solution.py:191
  152.1 24.0 %collective-permute-start.11 = (bf16[512,512]{1,0:T(8,128)(2,1)S(1)}, bf16[512,512]{1,0:T(8,128)(2,1)S(1)}, u32[]{:S(2)}, u32[]{:S(2)}) collective-permute-start(bf16[512,512]{1,0:T(8,128)(2,1)S(1)} %shard_map.57), channel_id=1, source_target_pairs={{1,0},{0,1},{3,2},{2,3},{5,4},{4,5},{7,6},{6,7},{9,8},{8,9},{11,10... | collective-permute-start | bytes 1572872 | tf_op jit(solution)/shard_map/ppermute | solution.py:191
  152.4 35.0 %collective-permute-start.12 = (bf16[512,512]{1,0:T(8,128)(2,1)S(1)}, bf16[512,512]{1,0:T(8,128)(2,1)S(1)}, u32[]{:S(2)}, u32[]{:S(2)}) collective-permute-start(bf16[512,512]{1,0:T(8,128)(2,1)S(1)} %shard_map.58), channel_id=1, source_target_pairs={{1,0},{0,1},{3,2},{2,3},{5,4},{4,5},{7,6},{6,7},{9,8},{8,9},{11,10... | collective-permute-start | bytes 1572872 | tf_op jit(solution)/shard_map/ppermute | solution.py:191
  167.1 26.1 %collective-permute-start.13 = (bf16[512,512]{1,0:T(8,128)(2,1)S(1)}, bf16[512,512]{1,0:T(8,128)(2,1)S(1)}, u32[]{:S(2)}, u32[]{:S(2)}) collective-permute-start(bf16[512,512]{1,0:T(8,128)(2,1)S(1)} %shard_map.59), channel_id=1, source_target_pairs={{1,0},{0,1},{3,2},{2,3},{5,4},{4,5},{7,6},{6,7},{9,8},{8,9},{11,10... | collective-permute-start | bytes 1572872 | tf_op jit(solution)/shard_map/ppermute | solution.py:191
